TPU v7x, 512 devices: a whole 4x4x16 slice. The times are simulated.
512 devices in a mesh: rows: 128 (over y_hi, z, x), cols: 4 (over y_lo, core).
Axes of the slice: x: 4, y: 4 (y_hi: 2, y_lo: 2; y = y_hi * 2 + y_lo), z: 16, core: 2. Of those that a mesh axis runs over, the one named last changes fastest.
Arguments:
- features: bfloat16 [524288, 256], P('rows', 'cols'), may hold values from -6 to 6
- weight: bfloat16 [256, 256], P(None, 'cols'), may hold values from -0.375 to 0.375
- tile_values: bfloat16 [11264, 128, 128], P('rows'), as said below
- tile_rows: int32 [11264], P('rows'), may hold values from 0 to 31
- tile_cols: int32 [11264], P('rows'), may hold values from 0 to 159, as said below
- tile_count: int32 [128], P('rows'), may hold values from 44 to 88, as said below
- cotangent: bfloat16 [524288, 256], P('rows', 'cols'), may hold values from -6 to 6
Outputs:
- output: bfloat16 [524288, 256], P('rows', 'cols')
- feature_grad: bfloat16 [524288, 256], P('rows', 'cols')
- weight_grad: float32 [256, 256], P(None, 'cols')
Inputs may be any that keep to these rules, and one draw needn't show every extreme that they name: `tile_count`: live tile slots of a partition, at least 44; some partition has all 88 slots live in every draw. `tile_cols`: slot s of a partition (counted from the partition's first slot) draws its source from the partition (s mod 5) - 2 steps away around the loop, so c div (32) = s mod 5. `tile_values`: edge weights are zero or positive.
All inputs are finite; a program needn't handle non-finite values.
Results may differ from a plain program's by a relative error of at most 0.02.
Values may be sent and summed in bfloat16 or wider, within the bound.
No kernel may reach another device: no remote copies, remote signals or barrier semaphores. Data moves between devices by JAX's collectives and lax.ppermute only.
A program may use at most 64 MiB of HBM per device.

v0:
```python
import jax
import jax.numpy as jnp
from jax import lax
from jax.sharding import PartitionSpec as P


def passed_along(value, axis, steps):
    count = lax.axis_size(axis)
    pairs = [(source, (source + steps) % count) for source in range(count)]
    return lax.ppermute(value, axis, pairs)


def silu_grad(value):
    sigmoid_val = jax.nn.sigmoid(value)
    return sigmoid_val * (1.0 + value * (1.0 - sigmoid_val))


def local(features, weight, tile_values, tile_rows, tile_cols, tile_count, cotangent):
    node_count, feat_cols = features.shape
    slot_count, tile_size = (tile_values.shape[0], tile_values.shape[1])
    block_count = node_count // tile_size
    block_ids = jnp.arange(block_count, dtype=jnp.int32)
    live_slots = (jnp.arange(slot_count, dtype=jnp.int32) < tile_count[0]).astype(jnp.float32)
    going_down = features
    going_up = features
    lower_blocks = []
    upper_blocks = []
    for section in range(2):
        going_down = passed_along(going_down, "rows", 1)
        lower_blocks.append(going_down)
        going_up = passed_along(going_up, "rows", -1)
        upper_blocks.append(going_up)
    band_rows = jnp.concatenate(
        [lower_blocks[1], lower_blocks[0], features, upper_blocks[0], upper_blocks[1]], 0
    )
    band_rows = band_rows.reshape(5 * block_count, tile_size, feat_cols)
    source = band_rows[tile_cols]
    products = (
        jnp.einsum("tij,tjf->tif", tile_values, source, preferred_element_type=jnp.float32)
        * live_slots[:, None, None]
    )
    row_select = (tile_rows[None, :] == block_ids[:, None]).astype(jnp.float32)
    hidden_part = (
        jnp.einsum("bt,tif->bif", row_select, products)
        .reshape(node_count, feat_cols)
        .astype(jnp.bfloat16)
    )
    hidden = lax.all_gather(hidden_part, "cols", axis=1, tiled=True)
    preact = jnp.dot(hidden, weight, preferred_element_type=jnp.float32)
    output = jax.nn.silu(preact).astype(jnp.bfloat16)
    grad_pre = (cotangent.astype(jnp.float32) * silu_grad(preact)).astype(jnp.bfloat16)
    total_nodes = node_count * lax.axis_size("rows")
    weight_term = lax.dot_general(
        hidden, grad_pre, (((0,), (0,)), ((), ())), preferred_element_type=jnp.float32
    )
    weight_grad = lax.psum(weight_term, "rows") * (1.0 / total_nodes**0.5)
    partial_terms = lax.dot_general(
        grad_pre, weight, (((1,), (1,)), ((), ())), preferred_element_type=jnp.float32
    )
    hidden_grad = lax.psum_scatter(
        partial_terms.astype(jnp.bfloat16), "cols", scatter_dimension=1, tiled=True
    )
    grad_blocks = hidden_grad.reshape(block_count, tile_size, feat_cols)
    grad_source = grad_blocks[tile_rows]
    contrib = (
        jnp.einsum("tji,tjf->tif", tile_values, grad_source, preferred_element_type=jnp.float32)
        * live_slots[:, None, None]
    )
    band_select = (
        tile_cols[None, :] == jnp.arange(5 * block_count, dtype=jnp.int32)[:, None]
    ).astype(jnp.float32)
    outgoing = jnp.einsum("ct,tif->cif", band_select, contrib).reshape(5, node_count, feat_cols)
    moving_up = outgoing[4]
    moving_down = outgoing[0]
    for section in range(2):
        moving_up = passed_along(moving_up.astype(jnp.bfloat16), "rows", 1).astype(moving_up.dtype)
        moving_down = passed_along(moving_down.astype(jnp.bfloat16), "rows", -1).astype(
            moving_down.dtype
        )
        if section == 0:
            moving_up = moving_up + outgoing[3]
            moving_down = moving_down + outgoing[1]
    gathered = outgoing[2] + moving_up + moving_down
    feature_grad = gathered.astype(jnp.bfloat16)
    return (output, feature_grad, weight_grad)


def solution(mesh):
    in_specs = (
        P("rows", "cols"),
        P(None, "cols"),
        P("rows", None, None),
        P("rows"),
        P("rows"),
        P("rows"),
        P("rows", "cols"),
    )
    out_specs = (P("rows", "cols"), P("rows", "cols"), P(None, "cols"))
    return jax.shard_map(local, mesh=mesh, in_specs=in_specs, out_specs=out_specs, check_vma=False)
```

profile of v0, /device:TPU:8, one launch (start us, length us, event | category | flops | bytes accessed | tf_op | source)
XLA Modules:
  0.0 1374.6 jit_solution(18113469015568557949)
XLA Ops:
  7.2 3.7 collective-permute-start
  10.9 13.9 %collective-permute-start.2 = (bf16[4096,64]{0,1:T(8,128)(2,1)}, bf16[4096,64]{0,1:T(8,128)(2,1)S(1)}, u32[]{:S(2)}, u32[]{:S(2)}) collective-permute-start(bf16[4096,64]{0,1:T(8,128)(2,1)} %param.7), channel_id=1, source_target_pairs={{0,508},{4,0},{8,4},{12,8},{16,12},{20,16},{24,20},{28,24},{32,28}... | collective-permute-start | bytes 1572872 | tf_op jit(solution)/shard_map/ppermute | solution.py:10
  24.8 10.2 collective-permute-done
  34.9 1.9 collective-permute-start.1
  38.2 9.6 collective-permute-start.3
  47.8 7.8 collective-permute-done.1
  55.7 1.1 constant_dynamic-update-slice_fusion.2
  56.9 1.3 collective-permute-done.3
  58.2 2.3 copy_bitcast_fusion
  60.5 3.7 gather_fusion
  64.1 3.5 multiply_bitcast_fusion.1
  67.6 1.0 fusion.4
  69.7 29.8 %all-gather.2.cloned.1.call-done = bf16[4096,256]{0,1:T(8,128)(2,1)} async-done(((bf16[4096,64]{0,1:T(8,128)(2,1)}), bf16[4096,256]{0,1:T(8,128)(2,1)}) %all-gather.2.cloned.1.call-update) | async-done | bytes 2097168 | tf_op jit(solution)/shard_map/all_gather | solution.py:48
  99.5 3.2 multiply_convert_fusion
  103.5 2.0 convolution_convert_fusion
  105.7 37.0 %reduce-scatter.2.cloned.1.call-done = bf16[4096,64]{0,1:T(8,128)(2,1)} async-done(((bf16[4096,256]{0,1:T(8,128)(2,1)}), bf16[4096,64]{0,1:T(8,128)(2,1)}) %reduce-scatter.2.cloned.1.call-update) | async-done | bytes 524304 | tf_op jit(solution)/shard_map/reduce_scatter | solution.py:60
  142.6 1.2 copy_bitcast_fusion.4
  143.8 1.9 gather_fusion.1
  145.7 2.3 multiply_bitcast_fusion
  148.0 1.6 fusion.19
  149.9 10.7 collective-permute-start.6
  160.8 1.9 collective-permute-start.4
  162.7 1.3 fusion.17
  164.0 8.0 collective-permute-done.6
  172.0 1.4 fusion.7
  173.4 10.1 collective-permute-start.7
  183.5 1.4 fusion.8
  184.9 1.9 collective-permute-start.5
  186.8 1.4 fusion.20
  188.2 1175.6 %all-reduce.2.cloned.1.call-done = f32[256,64]{0,1:T(8,128)} async-done(((f32[256,64]{0,1:T(8,128)}), f32[256,64]{0,1:T(8,128)}) %all-reduce.2.cloned.1.call-update) | async-done | bytes 65552 | tf_op jit(solution)/shard_map/psum | solution.py:56
  1363.8 1.5 broadcast_multiply_fusion
  1365.3 2.8 fusion.10
  (37 shorter events, 3.3 us)
Async XLA Ops:
  7.2 57.0 %copy-start = (bf16[88,128,128]{2,1,0:T(8,128)(2,1)S(1)}, bf16[88,128,128]{2,1,0:T(8,128)(2,1)}, u32[]{:S(2)}) copy-start(bf16[88,128,128]{2,1,0:T(8,128)(2,1)} %param.9) | copy-start | bytes 8650756
  7.2 92.3 %all-gather.2.cloned.1.call-start = ((), (), s32[]{:S(2)}) async-start(), calls=%async_computation.1 | async-start | bytes 2621440 | tf_op jit(solution)/shard_map/all_gather | solution.py:48
  7.2 27.7 %collective-permute-start = (bf16[4096,64]{0,1:T(8,128)(2,1)}, bf16[4096,64]{0,1:T(8,128)(2,1)S(1)}, u32[]{:S(2)}, u32[]{:S(2)}) collective-permute-start(bf16[4096,64]{0,1:T(8,128)(2,1)} %param.7), channel_id=1, source_target_pairs={{0,4},{4,8},{8,12},{12,16},{16,20},{20,24},{24,28},{28,32},{32,36}... | collective-permute-start | bytes 1572872 | tf_op jit(solution)/shard_map/ppermute | solution.py:10
  10.9 27.3 %collective-permute-start.2 = (bf16[4096,64]{0,1:T(8,128)(2,1)}, bf16[4096,64]{0,1:T(8,128)(2,1)S(1)}, u32[]{:S(2)}, u32[]{:S(2)}) collective-permute-start(bf16[4096,64]{0,1:T(8,128)(2,1)} %param.7), channel_id=1, source_target_pairs={{0,508},{4,0},{8,4},{12,8},{16,12},{20,16},{24,20},{28,24},{32,28}... | collective-permute-start | bytes 1572872 | tf_op jit(solution)/shard_map/ppermute | solution.py:10
  34.9 20.7 %collective-permute-start.1 = (bf16[4096,64]{0,1:T(8,128)(2,1)S(1)}, bf16[4096,64]{0,1:T(8,128)(2,1)S(1)}, u32[]{:S(2)}, u32[]{:S(2)}) collective-permute-start(bf16[4096,64]{0,1:T(8,128)(2,1)S(1)} %collective-permute-done), channel_id=1, source_target_pairs={{0,4},{4,8},{8,12},{12,16},{16,20},{20,24},{24,28},{28,32},{32,36}... | collective-permute-start | bytes 1572872 | tf_op jit(solution)/shard_map/ppermute | solution.py:10
  38.2 20.0 %collective-permute-start.3 = (bf16[4096,64]{0,1:T(8,128)(2,1)S(1)}, bf16[4096,64]{0,1:T(8,128)(2,1)S(1)}, u32[]{:S(2)}, u32[]{:S(2)}) collective-permute-start(bf16[4096,64]{0,1:T(8,128)(2,1)S(1)} %collective-permute-done.2), channel_id=1, source_target_pairs={{0,508},{4,0},{8,4},{12,8},{16,12},{20,16},{24,20},{28,24},{32,28}... | collective-permute-start | bytes 1572872 | tf_op jit(solution)/shard_map/ppermute | solution.py:10
  64.1 3.5 copy-start.5
  67.6 31.9 %copy-start.4 = (bf16[256,64]{0,1:T(8,128)(2,1)S(1)}, bf16[256,64]{0,1:T(8,128)(2,1)}, u32[]{:S(2)}) copy-start(bf16[256,64]{0,1:T(8,128)(2,1)} %param.8) | copy-start | bytes 98308
  69.7 72.9 %reduce-scatter.2.cloned.1.call-start = ((), (), s32[]{:S(2)}) async-start(), calls=%async_computation.2 | async-start | bytes 2621440 | tf_op jit(solution)/shard_map/reduce_scatter | solution.py:60
  102.7 0.8 copy-start.2
  105.6 1258.2 %all-reduce.2.cloned.1.call-start = ((), (), s32[]{:S(2)}) async-start(), calls=%async_computation.3 | async-start | bytes 131072 | tf_op jit(solution)/shard_map/psum | solution.py:56
  145.7 2.3 copy-start.6
  149.9 22.1 %collective-permute-start.6 = (bf16[4096,64]{0,1:T(8,128)(2,1)S(1)}, bf16[4096,64]{0,1:T(8,128)(2,1)S(1)}, u32[]{:S(2)}, u32[]{:S(2)}) collective-permute-start(bf16[4096,64]{0,1:T(8,128)(2,1)S(1)} %bitcast.83), channel_id=1, source_target_pairs={{0,508},{4,0},{8,4},{12,8},{16,12},{20,16},{24,20},{28,24},{32,28}... | collective-permute-start | bytes 1572872 | tf_op jit(solution)/shard_map/ppermute | solution.py:10
  160.8 22.7 %collective-permute-start.4 = (bf16[4096,64]{0,1:T(8,128)(2,1)S(1)}, bf16[4096,64]{0,1:T(8,128)(2,1)S(1)}, u32[]{:S(2)}, u32[]{:S(2)}) collective-permute-start(bf16[4096,64]{0,1:T(8,128)(2,1)S(1)} %bitcast.82), channel_id=1, source_target_pairs={{0,4},{4,8},{8,12},{12,16},{16,20},{20,24},{24,28},{28,32},{32,36}... | collective-permute-start | bytes 1572872 | tf_op jit(solution)/shard_map/ppermute | solution.py:10
  164.0 22.8 %copy-start.1 = (bf16[4096,256]{0,1:T(8,128)(2,1)S(1)}, bf16[4096,256]{0,1:T(8,128)(2,1)}, u32[]{:S(2)}) copy-start(bf16[4096,256]{0,1:T(8,128)(2,1)} %all-gather.2.cloned.1.call-done) | copy-start | bytes 6291460
  164.0 22.8 %copy-start.3 = (bf16[4096,64]{0,1:T(8,128)(2,1)S(1)}, bf16[4096,64]{0,1:T(8,128)(2,1)}, u32[]{:S(2)}) copy-start(bf16[4096,64]{0,1:T(8,128)(2,1)} %copy-done.2) | copy-start | bytes 1572868
  173.4 1191.9 %collective-permute-start.7 = (bf16[4096,64]{0,1:T(8,128)(2,1)}, bf16[4096,64]{0,1:T(8,128)(2,1)S(1)}, u32[]{:S(2)}, u32[]{:S(2)}) collective-permute-start(bf16[4096,64]{0,1:T(8,128)(2,1)} %fusion.7), channel_id=1, source_target_pairs={{0,508},{4,0},{8,4},{12,8},{16,12},{20,16},{24,20},{28,24},{32,28}... | collective-permute-start | bytes 1572872 | tf_op jit(solution)/shard_map/ppermute | solution.py:10
  184.9 1180.4 %collective-permute-start.5 = (bf16[4096,64]{0,1:T(8,128)(2,1)}, bf16[4096,64]{0,1:T(8,128)(2,1)}, u32[]{:S(2)}, u32[]{:S(2)}) collective-permute-start(bf16[4096,64]{0,1:T(8,128)(2,1)} %fusion.8), channel_id=1, source_target_pairs={{0,4},{4,8},{8,12},{12,16},{16,20},{20,24},{24,28},{28,32},{32,36}... | collective-permute-start | bytes 1572872 | tf_op jit(solution)/shard_map/ppermute | solution.py:10
Sparse Core Ops, SparseCore 0:
  69.8 29.6 all-gather.1
  105.7 36.8 reduce-scatter.1
  188.4 1175.4 all-reduce.1
where the time goes:
time: 1380 us; the launch traced here: 1370 us
  waiting for transfers between devices  1270 us (92%)
  starting transfers between devices  53.8 us (4%)
  matrix products  15 us (1%)
  between operations  14.6 us (1%)
  local copies, waits for them, and re-layouts  13.9 us (1%)
    psum x1, waiting for transfers between devices, local(): weight_grad = lax.psum(weight_term, 'rows') * (1.0 / total_nodes ** 0.5)  1180 us
    ppermute x8, starting transfers between devices, passed_along(): return lax.ppermute(value, axis, pairs)  53.7 us
    reduce_scatter x1, waiting for transfers between devices, local(): lax.psum_scatter(partial_terms.astype(jnp.bfloat16), 'cols', scatter_dime...  37 us
    all_gather x1, waiting for transfers between devices, local(): hidden = lax.all_gather(hidden_part, 'cols', axis=1, tiled=True)  29.8 us
  transfers between devices with their start and end apart: 11, of which 7 were waited for; matrix products, arithmetic and copies ran while one was open for 1% of the time, Pallas kernels for 0%

commit v1 on v0

--- a/solution.py
+++ b/solution.py
@@ -2,6 +2,10 @@
 import jax.numpy as jnp
 from jax import lax
 from jax.sharding import PartitionSpec as P
+
+
+def refer_run(own_rows, chip_axis):
+    return jax.lax.all_gather(own_rows, axis_name=chip_axis).sum(axis=0)
 
 
 def passed_along(value, axis, steps):
@@ -53,7 +57,7 @@
     weight_term = lax.dot_general(
         hidden, grad_pre, (((0,), (0,)), ((), ())), preferred_element_type=jnp.float32
     )
-    weight_grad = lax.psum(weight_term, "rows") * (1.0 / total_nodes**0.5)
+    weight_grad = refer_run(weight_term, "rows") * (1.0 / total_nodes**0.5)
     partial_terms = lax.dot_general(
         grad_pre, weight, (((1,), (1,)), ((), ())), preferred_element_type=jnp.float32
     )

time: 1380 us -> 404 us (0.29)
  the two profiles are of different devices: /device:TPU:8 before, /device:TPU:2 now
where the time goes in v1:
time: 404 us; the launch traced here: 403 us
  waiting for transfers between devices  305 us (75%)
  starting transfers between devices  43.5 us (11%)
  local copies, waits for them, and re-layouts  18 us (4%)
  matrix products  16.6 us (4%)
  between operations  14.6 us (4%)
  other arithmetic  5.66 us (1%)
    all_gather x1, waiting for transfers between devices, refer_run(): return jax.lax.all_gather(own_rows, axis_name=chip_axis).sum(axis=0)  189 us
    ppermute x8, waiting for transfers between devices, passed_along(): return lax.ppermute(value, axis, pairs)  44.2 us
    ppermute x8, starting transfers between devices, passed_along(): return lax.ppermute(value, axis, pairs)  43.4 us
    all_gather x1, waiting for transfers between devices, local(): hidden = lax.all_gather(hidden_part, 'cols', axis=1, tiled=True)  37.4 us
    reduce_scatter x1, waiting for transfers between devices, local(): lax.psum_scatter(partial_terms.astype(jnp.bfloat16), 'cols', scatter_dime...  34.1 us
    unnamed x16, local copies, waits for them, and re-layouts  8.51 us
  transfers between devices with their start and end apart: 11, of which 10 were waited for; matrix products, arithmetic and copies ran while one was open for 4% of the time, Pallas kernels for 0%

profile of v1, /device:TPU:2, one launch (start us, length us, event | category | flops | bytes accessed | tf_op | source)
XLA Modules:
  0.0 402.9 jit_solution(8314580286726726792)
XLA Ops:
  7.2 3.7 collective-permute-start
  10.9 6.3 %collective-permute-start.2 = (bf16[4096,64]{0,1:T(8,128)(2,1)}, bf16[4096,64]{0,1:T(8,128)(2,1)S(1)}, u32[]{:S(2)}, u32[]{:S(2)}) collective-permute-start(bf16[4096,64]{0,1:T(8,128)(2,1)} %param.7), channel_id=1, source_target_pairs={{0,508},{4,0},{8,4},{12,8},{16,12},{20,16},{24,20},{28,24},{32,28}... | collective-permute-start | bytes 1572872 | tf_op jit(solution)/shard_map/ppermute | solution.py:14
  17.2 6.0 %collective-permute-done = bf16[4096,64]{0,1:T(8,128)(2,1)S(1)} collective-permute-done((bf16[4096,64]{0,1:T(8,128)(2,1)}, bf16[4096,64]{0,1:T(8,128)(2,1)S(1)}, u32[]{:S(2)}, u32[]{:S(2)}) %collective-permute-start) | collective-permute-done | bytes 524320 | tf_op jit(solution)/shard_map/ppermute | solution.py:14
  23.3 3.4 collective-permute-start.1
  28.0 13.6 %collective-permute-start.3 = (bf16[4096,64]{0,1:T(8,128)(2,1)S(1)}, bf16[4096,64]{0,1:T(8,128)(2,1)S(1)}, u32[]{:S(2)}, u32[]{:S(2)}) collective-permute-start(bf16[4096,64]{0,1:T(8,128)(2,1)S(1)} %collective-permute-done.2), channel_id=1, source_target_pairs={{0,508},{4,0},{8,4},{12,8},{16,12},{20,16},{24,20},{28,24},{32,28}... | collective-permute-start | bytes 1572872 | tf_op jit(solution)/shard_map/ppermute | solution.py:14
  41.5 8.1 %collective-permute-done.1 = bf16[4096,64]{0,1:T(8,128)(2,1)S(1)} collective-permute-done((bf16[4096,64]{0,1:T(8,128)(2,1)S(1)}, bf16[4096,64]{0,1:T(8,128)(2,1)S(1)}, u32[]{:S(2)}, u32[]{:S(2)}) %collective-permute-start.1) | collective-permute-done | bytes 524320 | tf_op jit(solution)/shard_map/ppermute | solution.py:14
  49.7 1.1 constant_dynamic-update-slice_fusion.2
  50.8 1.3 collective-permute-done.3
  52.2 2.2 copy_bitcast_fusion
  54.4 3.7 gather_fusion
  58.1 3.5 multiply_bitcast_fusion.1
  61.6 1.0 fusion.4
  63.7 37.4 %all-gather.4.cloned.1.call-done = bf16[4096,256]{0,1:T(8,128)(2,1)} async-done(((bf16[4096,64]{0,1:T(8,128)(2,1)}), bf16[4096,256]{0,1:T(8,128)(2,1)}) %all-gather.4.cloned.1.call-update) | async-done | bytes 2097168 | tf_op jit(solution)/shard_map/all_gather | solution.py:52
  101.1 3.2 multiply_convert_fusion
  104.3 2.1 convolution_convert_fusion
  106.5 3.0 fusion.20
  109.6 34.1 %reduce-scatter.2.cloned.1.call-done = bf16[4096,64]{0,1:T(8,128)(2,1)} async-done(((bf16[4096,256]{0,1:T(8,128)(2,1)}), bf16[4096,64]{0,1:T(8,128)(2,1)}) %reduce-scatter.2.cloned.1.call-update) | async-done | bytes 524304 | tf_op jit(solution)/shard_map/reduce_scatter | solution.py:64
  143.6 1.2 copy_bitcast_fusion.4
  144.8 1.9 gather_fusion.1
  146.8 2.3 multiply_bitcast_fusion
  149.1 1.6 fusion.19
  150.9 2.5 collective-permute-start.6
  153.6 3.4 collective-permute-start.4
  157.3 9.4 %collective-permute-done.6 = bf16[4096,64]{0,1:T(8,128)(2,1)S(1)} collective-permute-done((bf16[4096,64]{0,1:T(8,128)(2,1)S(1)}, bf16[4096,64]{0,1:T(8,128)(2,1)S(1)}, u32[]{:S(2)}, u32[]{:S(2)}) %collective-permute-start.6) | collective-permute-done | bytes 524320 | tf_op jit(solution)/shard_map/ppermute | solution.py:14
  167.4 8.5 %collective-permute-start.7 = (bf16[4096,64]{0,1:T(8,128)(2,1)S(1)}, bf16[4096,64]{0,1:T(8,128)(2,1)S(1)}, u32[]{:S(2)}, u32[]{:S(2)}) collective-permute-start(bf16[4096,64]{0,1:T(8,128)(2,1)S(1)} %fusion.7), channel_id=1, source_target_pairs={{0,508},{4,0},{8,4},{12,8},{16,12},{20,16},{24,20},{28,24},{32,28}... | collective-permute-start | bytes 1572872 | tf_op jit(solution)/shard_map/ppermute | solution.py:14
  176.7 2.1 collective-permute-start.5
  178.8 7.8 %collective-permute-done.7 = bf16[4096,64]{0,1:T(8,128)(2,1)S(1)} collective-permute-done((bf16[4096,64]{0,1:T(8,128)(2,1)S(1)}, bf16[4096,64]{0,1:T(8,128)(2,1)S(1)}, u32[]{:S(2)}, u32[]{:S(2)}) %collective-permute-start.7) | collective-permute-done | bytes 524320 | tf_op jit(solution)/shard_map/ppermute | solution.py:14
  186.6 11.4 %collective-permute-done.5 = bf16[4096,64]{0,1:T(8,128)(2,1)S(1)} collective-permute-done((bf16[4096,64]{0,1:T(8,128)(2,1)S(1)}, bf16[4096,64]{0,1:T(8,128)(2,1)S(1)}, u32[]{:S(2)}, u32[]{:S(2)}) %collective-permute-start.5) | collective-permute-done | bytes 524320 | tf_op jit(solution)/shard_map/ppermute | solution.py:14
  198.1 1.5 fusion.10
  199.5 188.8 %all-gather.6.cloned.1.call-done = f32[32768,64]{0,1:T(8,128)} async-done(((f32[256,64]{0,1:T(8,128)}), f32[32768,64]{0,1:T(8,128)}) %all-gather.6.cloned.1.call-update) | async-done | bytes 8388624 | tf_op jit(solution)/shard_map/all_gather | solution.py:8
  388.3 5.9 %copy.23 = f32[8,8,128,256]{3,2,1,0:T(8,128)S(1)} copy(f32[8,8,128,256]{3,1,2,0:T(8,128)} %bitcast.80) | data formatting | bytes 16777216
  394.2 1.5 bitcast_reduce_fusion
  (33 shorter events, 4.9 us)
Async XLA Ops:
  7.2 50.9 %copy-start = (bf16[88,128,128]{2,1,0:T(8,128)(2,1)S(1)}, bf16[88,128,128]{2,1,0:T(8,128)(2,1)}, u32[]{:S(2)}) copy-start(bf16[88,128,128]{2,1,0:T(8,128)(2,1)} %param.9) | copy-start | bytes 8650756
  7.2 93.9 %all-gather.4.cloned.1.call-start = ((), (), s32[]{:S(2)}) async-start(), calls=%async_computation.1 | async-start | bytes 2621440 | tf_op jit(solution)/shard_map/all_gather | solution.py:52
  7.2 16.0 %collective-permute-start = (bf16[4096,64]{0,1:T(8,128)(2,1)}, bf16[4096,64]{0,1:T(8,128)(2,1)S(1)}, u32[]{:S(2)}, u32[]{:S(2)}) collective-permute-start(bf16[4096,64]{0,1:T(8,128)(2,1)} %param.7), channel_id=1, source_target_pairs={{0,4},{4,8},{8,12},{12,16},{16,20},{20,24},{24,28},{28,32},{32,36}... | collective-permute-start | bytes 1572872 | tf_op jit(solution)/shard_map/ppermute | solution.py:14
  10.9 17.1 %collective-permute-start.2 = (bf16[4096,64]{0,1:T(8,128)(2,1)}, bf16[4096,64]{0,1:T(8,128)(2,1)S(1)}, u32[]{:S(2)}, u32[]{:S(2)}) collective-permute-start(bf16[4096,64]{0,1:T(8,128)(2,1)} %param.7), channel_id=1, source_target_pairs={{0,508},{4,0},{8,4},{12,8},{16,12},{20,16},{24,20},{28,24},{32,28}... | collective-permute-start | bytes 1572872 | tf_op jit(solution)/shard_map/ppermute | solution.py:14
  23.3 26.4 %collective-permute-start.1 = (bf16[4096,64]{0,1:T(8,128)(2,1)S(1)}, bf16[4096,64]{0,1:T(8,128)(2,1)S(1)}, u32[]{:S(2)}, u32[]{:S(2)}) collective-permute-start(bf16[4096,64]{0,1:T(8,128)(2,1)S(1)} %collective-permute-done), channel_id=1, source_target_pairs={{0,4},{4,8},{8,12},{12,16},{16,20},{20,24},{24,28},{28,32},{32,36}... | collective-permute-start | bytes 1572872 | tf_op jit(solution)/shard_map/ppermute | solution.py:14
  28.0 24.2 %collective-permute-start.3 = (bf16[4096,64]{0,1:T(8,128)(2,1)S(1)}, bf16[4096,64]{0,1:T(8,128)(2,1)S(1)}, u32[]{:S(2)}, u32[]{:S(2)}) collective-permute-start(bf16[4096,64]{0,1:T(8,128)(2,1)S(1)} %collective-permute-done.2), channel_id=1, source_target_pairs={{0,508},{4,0},{8,4},{12,8},{16,12},{20,16},{24,20},{28,24},{32,28}... | collective-permute-start | bytes 1572872 | tf_op jit(solution)/shard_map/ppermute | solution.py:14
  58.1 3.5 copy-start.2
  61.6 39.5 %copy-start.1 = (bf16[256,64]{0,1:T(8,128)(2,1)S(1)}, bf16[256,64]{0,1:T(8,128)(2,1)}, u32[]{:S(2)}) copy-start(bf16[256,64]{0,1:T(8,128)(2,1)} %param.8) | copy-start | bytes 98308
  63.7 80.0 %reduce-scatter.2.cloned.1.call-start = ((), (), s32[]{:S(2)}) async-start(), calls=%async_computation.2 | async-start | bytes 2621440 | tf_op jit(solution)/shard_map/reduce_scatter | solution.py:64
  106.5 281.9 %all-gather.6.cloned.1.call-start = ((), (), s32[]{:S(2)}) async-start(), calls=%async_computation.3 | async-start | bytes 8454144 | tf_op jit(solution)/shard_map/all_gather | solution.py:8
  146.8 2.3 copy-start.3
  150.9 15.8 %collective-permute-start.6 = (bf16[4096,64]{0,1:T(8,128)(2,1)S(1)}, bf16[4096,64]{0,1:T(8,128)(2,1)S(1)}, u32[]{:S(2)}, u32[]{:S(2)}) collective-permute-start(bf16[4096,64]{0,1:T(8,128)(2,1)S(1)} %bitcast.89), channel_id=1, source_target_pairs={{0,508},{4,0},{8,4},{12,8},{16,12},{20,16},{24,20},{28,24},{32,28}... | collective-permute-start | bytes 1572872 | tf_op jit(solution)/shard_map/ppermute | solution.py:14
  153.6 22.4 %collective-permute-start.4 = (bf16[4096,64]{0,1:T(8,128)(2,1)S(1)}, bf16[4096,64]{0,1:T(8,128)(2,1)S(1)}, u32[]{:S(2)}, u32[]{:S(2)}) collective-permute-start(bf16[4096,64]{0,1:T(8,128)(2,1)S(1)} %bitcast.88), channel_id=1, source_target_pairs={{0,4},{4,8},{8,12},{12,16},{16,20},{20,24},{24,28},{28,32},{32,36}... | collective-permute-start | bytes 1572872 | tf_op jit(solution)/shard_map/ppermute | solution.py:14
  167.4 19.2 %collective-permute-start.7 = (bf16[4096,64]{0,1:T(8,128)(2,1)S(1)}, bf16[4096,64]{0,1:T(8,128)(2,1)S(1)}, u32[]{:S(2)}, u32[]{:S(2)}) collective-permute-start(bf16[4096,64]{0,1:T(8,128)(2,1)S(1)} %fusion.7), channel_id=1, source_target_pairs={{0,508},{4,0},{8,4},{12,8},{16,12},{20,16},{24,20},{28,24},{32,28}... | collective-permute-start | bytes 1572872 | tf_op jit(solution)/shard_map/ppermute | solution.py:14
  176.7 21.4 %collective-permute-start.5 = (bf16[4096,64]{0,1:T(8,128)(2,1)S(1)}, bf16[4096,64]{0,1:T(8,128)(2,1)S(1)}, u32[]{:S(2)}, u32[]{:S(2)}) collective-permute-start(bf16[4096,64]{0,1:T(8,128)(2,1)S(1)} %fusion.8), channel_id=1, source_target_pairs={{0,4},{4,8},{8,12},{12,16},{16,20},{20,24},{24,28},{28,32},{32,36}... | collective-permute-start | bytes 1572872 | tf_op jit(solution)/shard_map/ppermute | solution.py:14
Sparse Core Ops, SparseCore 0:
  63.8 37.2 all-gather.3
  106.6 37.0 reduce-scatter.1
  149.3 238.9 all-gather.5
